TPU v7x, 512 devices: a whole 4x8x8 slice. The times are simulated.
512 devices in a mesh: asset: 64 (over y, z), rhs: 8 (over x, core).
Axes of the slice: x: 4, y: 8, z: 8, core: 2. Of those that a mesh axis runs over, the one named last changes fastest.
Arguments:
- targets: float32 [65536, 1024], P('asset', 'rhs'), may hold values from -27 to 27
- ridge: float32 [65536], P('asset'), may hold values from 0.8 to 2.5
- blocks: bfloat16 [512, 16, 128, 128], P('asset', None, 'rhs'), may hold values from -0.046875 to 0.046875
- col_index: int32 [512, 16], P('asset'), may hold values from 0 to 511, as said below
- row_length: int32 [512], P('asset'), may hold values from 8 to 16, as said below
Outputs:
- solution: float32 [65536, 1024], P('asset', 'rhs')
- residual: float32 [65536, 1024], P('asset', 'rhs')
Inputs may be any that keep to these rules, and one draw needn't show every extreme that they name: `col_index`: the block columns of row i are distinct and lie within 8 blocks of i, counted cyclically modulo 512; slots at or past row_length[i] hold such columns too and are ignored. `row_length`: each aligned group of 8 block rows holds at least one row with 16 used slots.
All inputs are finite; a program needn't handle non-finite values.
Results may differ from a plain program's by a relative error of at most 0.0075.
Values may be sent and summed in bfloat16 or wider, within the bound.
A program may use at most 64 MiB of HBM per device.

v0:
```python
import jax
import jax.numpy as jnp
from jax import lax
from jax.sharding import PartitionSpec as P

ITERS = 3


def from_behind(block, axis, distance):
    devices = range(lax.axis_size(axis))
    route = [((i - distance) % len(devices), i) for i in devices]
    return lax.ppermute(block, axis, route)


def extended_2(shard, sides, width):
    for axis, dim in sides:
        devices, length = (lax.axis_size(axis), shard.shape[dim])
        up = [(i, (i + 1) % devices) for i in range(devices)]
        down = [(j, i) for i, j in up]
        last = lax.slice_in_dim(shard, length - width, length, axis=dim)
        first = lax.slice_in_dim(shard, 0, width, axis=dim)
        before = lax.ppermute(last, axis, up)
        after = lax.ppermute(first, axis, down)
        shard = jnp.concatenate([before, shard, after], axis=dim)
    return shard


def shards(targets, ridge, blocks, col_index, row_length):
    rows = col_index.shape[0]
    slots = col_index.shape[1]
    width = blocks.shape[3]
    cols = targets.shape[1]
    total = rows * lax.axis_size("asset")
    start = lax.axis_index("asset") * rows
    used = jnp.arange(slots)[None, :] < row_length[:, None]
    masked_shard = blocks * used[:, :, None, None].astype(jnp.bfloat16)
    local_pos = (col_index - start + rows) % total
    onehot = (local_pos[None, :, :] == jnp.arange(3 * rows, dtype=jnp.int32)[:, None, None]).astype(
        jnp.bfloat16
    )
    own_blocks = lax.all_gather(masked_shard, "rhs", axis=2, tiled=True)
    weave = jnp.einsum(
        "cik,ikab->ciab", onehot, own_blocks, preferred_element_type=jnp.float32
    ).astype(jnp.bfloat16)

    def squares(values):
        return lax.psum(jnp.sum(values * values, axis=0), "asset")

    solution = jnp.zeros_like(targets)
    residual = targets
    direction = targets
    norm_now = squares(residual)
    for step in range(ITERS):
        rounded = direction.astype(jnp.bfloat16)
        operate_extended = extended_2(rounded, (("asset", 0),), rows * width)
        operate_extended = operate_extended.reshape(3 * rows, width, cols)
        picked = jnp.take(operate_extended, local_pos, axis=0)
        forward = jnp.einsum(
            "ikab,ikbn->ian", own_blocks, picked, preferred_element_type=jnp.float32
        )
        slab = jnp.einsum(
            "qjpt,jpu->qtu",
            weave,
            operate_extended[rows : 2 * rows],
            preferred_element_type=jnp.float32,
        )
        from_upper = from_behind(slab[:rows].astype(jnp.bfloat16), "asset", -1).astype(jnp.float32)
        from_lower = from_behind(slab[2 * rows :].astype(jnp.bfloat16), "asset", 1).astype(
            jnp.float32
        )
        backward = slab[rows : 2 * rows] + from_upper + from_lower
        image = ridge[:, None] * direction + 0.5 * (forward + backward).reshape(rows * width, cols)
        curve = lax.psum(jnp.sum(direction * image, axis=0), "asset")
        alpha = norm_now / curve
        solution = solution + alpha * direction
        residual = residual - alpha * image
        norm_next = squares(residual)
        direction = residual + norm_next / norm_now * direction
        norm_now = norm_next
    return (solution, residual)


def solution(mesh):
    return jax.shard_map(
        shards,
        mesh=mesh,
        in_specs=(
            P("asset", "rhs"),
            P("asset"),
            P("asset", None, "rhs", None),
            P("asset", None),
            P("asset"),
        ),
        out_specs=(P("asset", "rhs"), P("asset", "rhs")),
        check_vma=False,
    )
```

profile of v0, /device:TPU:2, one launch (start us, length us, event | category | flops | bytes accessed | tf_op | source)
XLA Modules:
  0.0 876.3 jit_solution(18036171837793183966)
XLA Ops:
  11.1 13.9 %collective-permute-start.1 = (bf16[1024,128]{1,0:T(8,128)(2,1)S(1)}, bf16[1024,128]{1,0:T(8,128)(2,1)S(1)}, u32[]{:S(2)}, u32[]{:S(2)}) collective-permute-start(bf16[1024,128]{1,0:T(8,128)(2,1)S(1)} %convert_element_type.49), channel_id=1, source_target_pairs={{8,0},{16,8},{24,16},{32,24},{40,32},{48,40},{56,48},{64,56},{72,6... | collective-permute-start | bytes 786440 | tf_op jit(solution)/shard_map/ppermute | solution.py:23
  27.7 28.8 %all-gather.2.cloned.1.call-done = bf16[8,16,128,128]{3,2,1,0:T(8,128)(2,1)} async-done(((bf16[8,16,16,128]{3,2,1,0:T(8,128)(2,1)}), bf16[8,16,128,128]{3,2,1,0:T(8,128)(2,1)}) %all-gather.2.cloned.1.call-update) | async-done | bytes 4194320 | tf_op jit(solution)/shard_map/all_gather | solution.py:41
  56.4 8.0 convert_bitcast_fusion
  64.4 9.0 %copy.8 = bf16[24,8,128,128]{2,3,1,0:T(8,128)(2,1)} copy(bf16[24,8,128,128]{3,0,2,1:T(8,128)(2,1)} %convert_bitcast_fusion) | data formatting | bytes 12582912 | tf_op jit(solution)/shard_map/convert_element_type | solution.py:44
  73.5 4.6 fusion.53
  78.8 3.5 collective-permute-start.3
  82.3 6.5 collective-permute-start.2
  88.9 3.1 gather_fusion
  94.8 4.9 fusion.33
  100.0 143.9 %all-reduce = (f32[128]{0:T(128)S(1)}, f32[128]{0:T(128)S(1)}) all-reduce(f32[128]{0:T(128)S(1)} %get-tuple-element.4, f32[128]{0:T(128)S(1)} %get-tuple-element.3), channel_id=1, replica_groups=mesh['asset'=64,'rhs'=8] {'asset'}, use_global_device_ids=true, to_apply=%region_1.2 | all-reduce | flops 256 | bytes 2048 | tf_op jit(solution)/shard_map/psum | solution.py:47
  244.1 138.3 %psum.44 = f32[128]{0:T(128)S(1)} all-reduce(f32[128]{0:T(128)S(1)} %multiply_reduce_fusion.3), channel_id=1, replica_groups=mesh['asset'=64,'rhs'=8] {'asset'}, use_global_device_ids=true, to_apply=%region_5.7 | all-reduce | flops 128 | bytes 1024 | tf_op jit(solution)/shard_map/psum | solution.py:47
  382.6 3.7 collective-permute-start.5
  388.5 5.7 fusion.54
  394.3 3.7 collective-permute-start.7
  397.9 5.7 collective-permute-start.6
  407.3 4.9 fusion.30
  412.5 143.7 %psum.45 = f32[128]{0:T(128)S(1)} all-reduce(f32[128]{0:T(128)S(1)} %multiply_reduce_fusion.2), channel_id=1, replica_groups=mesh['asset'=64,'rhs'=8] {'asset'}, use_global_device_ids=true, to_apply=%region_7.9 | all-reduce | flops 128 | bytes 1024 | tf_op jit(solution)/shard_map/psum | solution.py:73
  556.5 138.0 %psum.46 = f32[128]{0:T(128)S(1)} all-reduce(f32[128]{0:T(128)S(1)} %get-tuple-element.7), channel_id=1, replica_groups=mesh['asset'=64,'rhs'=8] {'asset'}, use_global_device_ids=true, to_apply=%region_9.11 | all-reduce | flops 128 | bytes 1024 | tf_op jit(solution)/shard_map/psum | solution.py:47
  694.5 3.9 collective-permute-start.9
  700.4 5.7 fusion.55
  706.1 3.9 collective-permute-start.11
  710.1 5.3 collective-permute-start.10
  719.2 5.0 fusion.27
  724.4 143.9 %psum.47 = f32[128]{0:T(128)S(1)} all-reduce(f32[128]{0:T(128)S(1)} %multiply_reduce_fusion), channel_id=1, replica_groups=mesh['asset'=64,'rhs'=8] {'asset'}, use_global_device_ids=true, to_apply=%region_11.13 | all-reduce | flops 128 | bytes 1024 | tf_op jit(solution)/shard_map/psum | solution.py:73
  (49 shorter events, 24.5 us)
Async XLA Ops:
  7.2 49.3 %all-gather.2.cloned.1.call-start = ((), (), s32[]{:S(2)}) async-start(), calls=%async_computation | async-start | bytes 4718592 | tf_op jit(solution)/shard_map/all_gather | solution.py:41
  11.1 77.8 %collective-permute-start.1 = (bf16[1024,128]{1,0:T(8,128)(2,1)S(1)}, bf16[1024,128]{1,0:T(8,128)(2,1)S(1)}, u32[]{:S(2)}, u32[]{:S(2)}) collective-permute-start(bf16[1024,128]{1,0:T(8,128)(2,1)S(1)} %convert_element_type.49), channel_id=1, source_target_pairs={{8,0},{16,8},{24,16},{32,24},{40,32},{48,40},{56,48},{64,56},{72,6... | collective-permute-start | bytes 786440 | tf_op jit(solution)/shard_map/ppermute | solution.py:23
  24.9 63.9 %collective-permute-start = (bf16[1024,128]{1,0:T(8,128)(2,1)S(1)}, bf16[1024,128]{1,0:T(8,128)(2,1)S(1)}, u32[]{:S(2)}, u32[]{:S(2)}) collective-permute-start(bf16[1024,128]{1,0:T(8,128)(2,1)S(1)} %convert_element_type.49), channel_id=1, source_target_pairs={{0,8},{8,16},{16,24},{24,32},{32,40},{40,48},{48,56},{56,64},{64,7... | collective-permute-start | bytes 786440 | tf_op jit(solution)/shard_map/ppermute | solution.py:22
  78.8 15.2 %collective-permute-start.3 = (bf16[8,128,128]{2,1,0:T(8,128)(2,1)}, bf16[8,128,128]{2,1,0:T(8,128)(2,1)}, u32[]{:S(2)}, u32[]{:S(2)}) collective-permute-start(bf16[8,128,128]{2,1,0:T(8,128)(2,1)} %get-tuple-element.20), channel_id=1, source_target_pairs={{504,0},{0,8},{8,16},{16,24},{24,32},{32,40},{40,48},{48,56},{56,6... | collective-permute-start | bytes 786440 | tf_op jit(solution)/shard_map/ppermute | solution.py:12
  82.3 12.5 %collective-permute-start.2 = (bf16[8,128,128]{2,1,0:T(8,128)(2,1)S(1)}, bf16[8,128,128]{2,1,0:T(8,128)(2,1)}, u32[]{:S(2)}, u32[]{:S(2)}) collective-permute-start(bf16[8,128,128]{2,1,0:T(8,128)(2,1)S(1)} %get-tuple-element.19), channel_id=1, source_target_pairs={{8,0},{16,8},{24,16},{32,24},{40,32},{48,40},{56,48},{64,56},{72,6... | collective-permute-start | bytes 786440 | tf_op jit(solution)/shard_map/ppermute | solution.py:12
  94.8 4.9 copy-start
  94.8 5.0 copy-start.1
  382.6 21.0 %collective-permute-start.5 = (bf16[1024,128]{1,0:T(8,128)(2,1)S(1)}, bf16[1024,128]{1,0:T(8,128)(2,1)S(1)}, u32[]{:S(2)}, u32[]{:S(2)}) collective-permute-start(bf16[1024,128]{1,0:T(8,128)(2,1)S(1)} %get-tuple-element.9), channel_id=1, source_target_pairs={{8,0},{16,8},{24,16},{32,24},{40,32},{48,40},{56,48},{64,56},{72,6... | collective-permute-start | bytes 786440 | tf_op jit(solution)/shard_map/ppermute | solution.py:23
  386.3 17.3 %collective-permute-start.4 = (bf16[1024,128]{1,0:T(8,128)(2,1)S(1)}, bf16[1024,128]{1,0:T(8,128)(2,1)S(1)}, u32[]{:S(2)}, u32[]{:S(2)}) collective-permute-start(bf16[1024,128]{1,0:T(8,128)(2,1)S(1)} %get-tuple-element.9), channel_id=1, source_target_pairs={{0,8},{8,16},{16,24},{24,32},{32,40},{40,48},{48,56},{56,64},{64,7... | collective-permute-start | bytes 786440 | tf_op jit(solution)/shard_map/ppermute | solution.py:22
  394.3 12.6 %collective-permute-start.7 = (bf16[8,128,128]{2,1,0:T(8,128)(2,1)S(1)}, bf16[8,128,128]{2,1,0:T(8,128)(2,1)S(1)}, u32[]{:S(2)}, u32[]{:S(2)}) collective-permute-start(bf16[8,128,128]{2,1,0:T(8,128)(2,1)S(1)} %get-tuple-element.18), channel_id=1, source_target_pairs={{504,0},{0,8},{8,16},{16,24},{24,32},{32,40},{40,48},{48,56},{56,6... | collective-permute-start | bytes 786440 | tf_op jit(solution)/shard_map/ppermute | solution.py:12
  397.9 9.4 %collective-permute-start.6 = (bf16[8,128,128]{2,1,0:T(8,128)(2,1)S(1)}, bf16[8,128,128]{2,1,0:T(8,128)(2,1)S(1)}, u32[]{:S(2)}, u32[]{:S(2)}) collective-permute-start(bf16[8,128,128]{2,1,0:T(8,128)(2,1)S(1)} %get-tuple-element.17), channel_id=1, source_target_pairs={{8,0},{16,8},{24,16},{32,24},{40,32},{48,40},{56,48},{64,56},{72,6... | collective-permute-start | bytes 786440 | tf_op jit(solution)/shard_map/ppermute | solution.py:12
  694.5 20.8 %collective-permute-start.9 = (bf16[1024,128]{1,0:T(8,128)(2,1)S(1)}, bf16[1024,128]{1,0:T(8,128)(2,1)S(1)}, u32[]{:S(2)}, u32[]{:S(2)}) collective-permute-start(bf16[1024,128]{1,0:T(8,128)(2,1)S(1)} %fusion.34), channel_id=1, source_target_pairs={{8,0},{16,8},{24,16},{32,24},{40,32},{48,40},{56,48},{64,56},{72,6... | collective-permute-start | bytes 786440 | tf_op jit(solution)/shard_map/ppermute | solution.py:23
  698.4 16.9 %collective-permute-start.8 = (bf16[1024,128]{1,0:T(8,128)(2,1)S(1)}, bf16[1024,128]{1,0:T(8,128)(2,1)S(1)}, u32[]{:S(2)}, u32[]{:S(2)}) collective-permute-start(bf16[1024,128]{1,0:T(8,128)(2,1)S(1)} %fusion.34), channel_id=1, source_target_pairs={{0,8},{8,16},{16,24},{24,32},{32,40},{40,48},{48,56},{56,64},{64,7... | collective-permute-start | bytes 786440 | tf_op jit(solution)/shard_map/ppermute | solution.py:22
  706.1 12.3 %collective-permute-start.11 = (bf16[8,128,128]{2,1,0:T(8,128)(2,1)S(1)}, bf16[8,128,128]{2,1,0:T(8,128)(2,1)}, u32[]{:S(2)}, u32[]{:S(2)}) collective-permute-start(bf16[8,128,128]{2,1,0:T(8,128)(2,1)S(1)} %get-tuple-element.16), channel_id=1, source_target_pairs={{504,0},{0,8},{8,16},{16,24},{24,32},{32,40},{40,48},{48,56},{56,6... | collective-permute-start | bytes 786440 | tf_op jit(solution)/shard_map/ppermute | solution.py:12
  710.1 9.1 %collective-permute-start.10 = (bf16[8,128,128]{2,1,0:T(8,128)(2,1)S(1)}, bf16[8,128,128]{2,1,0:T(8,128)(2,1)}, u32[]{:S(2)}, u32[]{:S(2)}) collective-permute-start(bf16[8,128,128]{2,1,0:T(8,128)(2,1)S(1)} %get-tuple-element.15), channel_id=1, source_target_pairs={{8,0},{16,8},{24,16},{32,24},{40,32},{48,40},{56,48},{64,56},{72,6... | collective-permute-start | bytes 786440 | tf_op jit(solution)/shard_map/ppermute | solution.py:12
Sparse Core Ops, SparseCore 0:
  10.7 45.6 all-gather.1
where the time goes:
time: 877 us; the launch traced here: 876 us
  blocking collectives  708 us (81%)
  starting transfers between devices  56 us (6%)
  matrix products  38.9 us (4%)
  waiting for transfers between devices  32.9 us (4%)
  local copies, waits for them, and re-layouts  19.2 us (2%)
  between operations  14.3 us (2%)
    psum x3, blocking collectives, squares(): return lax.psum(jnp.sum(values * values, axis=0), 'asset')  420 us
    psum x2, blocking collectives, shards(): curve = lax.psum(jnp.sum(direction * image, axis=0), 'asset')  288 us
    all_gather x1, waiting for transfers between devices, shards(): own_blocks = lax.all_gather(masked_shard, 'rhs', axis=2, tiled=True)  28.8 us
    ppermute x6, starting transfers between devices, from_behind(): return lax.ppermute(block, axis, route)  28.5 us
    ppermute x3, starting transfers between devices, extended_2(): after = lax.ppermute(first, axis, down)  21.4 us
  transfers between devices with their start and end apart: 13, of which 5 were waited for; matrix products, arithmetic and copies ran while one was open for 5% of the time, Pallas kernels for 0%

commit v1 on v0

--- a/solution.py
+++ b/solution.py
@@ -44,7 +44,10 @@
     ).astype(jnp.bfloat16)
 
     def squares(values):
-        return lax.psum(jnp.sum(values * values, axis=0), "asset")
+        _register_results = lambda shard_in: jnp.sum(
+            lax.all_gather(shard_in, axis_name="asset"), axis=0
+        )
+        return _register_results(jnp.sum(values * values, axis=0))
 
     solution = jnp.zeros_like(targets)
     residual = targets

time: 877 us -> 721 us (0.82)
  the two profiles are of different devices: /device:TPU:2 before, /device:TPU:4 now
where the time goes in v1:
time: 721 us; the launch traced here: 720 us
  blocking collectives  550 us (76%)
  starting transfers between devices  57.3 us (8%)
  matrix products  39 us (5%)
  waiting for transfers between devices  32.9 us (5%)
  local copies, waits for them, and re-layouts  19.2 us (3%)
  between operations  14.3 us (2%)
  other arithmetic  7.59 us (1%)
    psum x3, blocking collectives, shards(): curve = lax.psum(jnp.sum(direction * image, axis=0), 'asset')  427 us
    all_gather x3, blocking collectives, squares(): lax.all_gather(shard_in, axis_name='asset')  123 us
    all_gather x1, waiting for transfers between devices, shards(): own_blocks = lax.all_gather(masked_shard, 'rhs', axis=2, tiled=True)  28.8 us
    ppermute x6, starting transfers between devices, from_behind(): return lax.ppermute(block, axis, route)  28.5 us
    ppermute x3, starting transfers between devices, extended_2(): after = lax.ppermute(first, axis, down)  22.4 us
    dot_general x3, matrix products, shards(): jnp.einsum('qjpt,jpu->qtu', weave, operate_extended[rows:2 * rows], prefe...  16 us
    dot_general x3, matrix products, shards(): jnp.einsum('ikab,ikbn->ian', own_blocks, picked, preferred_element_type=j...  14.9 us
  transfers between devices with their start and end apart: 13, of which 5 were waited for; matrix products, arithmetic and copies ran while one was open for 6% of the time, Pallas kernels for 0%

profile of v1, /device:TPU:4, one launch (start us, length us, event | category | flops | bytes accessed | tf_op | source)
XLA Modules:
  0.0 720.5 jit_solution(11352499120608561643)
XLA Ops:
  11.1 13.9 %collective-permute-start.1 = (bf16[1024,128]{1,0:T(8,128)(2,1)S(1)}, bf16[1024,128]{1,0:T(8,128)(2,1)S(1)}, u32[]{:S(2)}, u32[]{:S(2)}) collective-permute-start(bf16[1024,128]{1,0:T(8,128)(2,1)S(1)} %convert_element_type.49), channel_id=1, source_target_pairs={{8,0},{16,8},{24,16},{32,24},{40,32},{48,40},{56,48},{64,56},{72,6... | collective-permute-start | bytes 786440 | tf_op jit(solution)/shard_map/ppermute | solution.py:23
  27.7 28.8 %all-gather.8.cloned.1.call-done = bf16[8,16,128,128]{3,2,1,0:T(8,128)(2,1)} async-done(((bf16[8,16,16,128]{3,2,1,0:T(8,128)(2,1)}), bf16[8,16,128,128]{3,2,1,0:T(8,128)(2,1)}) %all-gather.8.cloned.1.call-update) | async-done | bytes 4194320 | tf_op jit(solution)/shard_map/all_gather | solution.py:41
  56.4 8.0 %convert_bitcast_fusion = bf16[24,8,128,128]{3,0,2,1:T(8,128)(2,1)} fusion(bf16[8,16,128,128]{3,2,1,0:T(8,128)(2,1)} %all-gather.8.cloned.1.call-done, s32[8,16]{1,0:T(8,128)S(1)} %get-tuple-element.10), kind=kOutput, calls=%fused_computation.3 | convolution fusion | flops 103812096 | bytes 10486272 | tf_op jit(solution)/shard_map/cik,ikab->ciab/dot_general | solution.py:42
  64.4 9.0 %copy.12 = bf16[24,8,128,128]{2,3,1,0:T(8,128)(2,1)} copy(bf16[24,8,128,128]{3,0,2,1:T(8,128)(2,1)} %convert_bitcast_fusion) | data formatting | bytes 12582912 | tf_op jit(solution)/shard_map/convert_element_type | solution.py:44
  73.5 4.6 fusion.53
  78.8 3.5 collective-permute-start.3
  82.3 6.5 collective-permute-start.2
  88.9 3.1 gather_fusion
  94.8 4.9 fusion.33
  100.0 45.1 %all-gather.3 = f32[64,1,128]{2,1,0:T(1,128)S(1)} all-gather(f32[1,1,128]{2,1,0:T(1,128)S(1)} %bitcast.94), channel_id=2, replica_groups=mesh['asset'=64,'rhs'=8] {'asset'}, dimensions={0}, use_global_device_ids=true | all-gather | bytes 33280 | tf_op jit(solution)/shard_map/all_gather | solution.py:48
  145.1 139.1 %psum.21 = f32[128]{0:T(128)S(1)} all-reduce(f32[128]{0:T(128)S(1)} %get-tuple-element.3), channel_id=1, replica_groups=mesh['asset'=64,'rhs'=8] {'asset'}, use_global_device_ids=true, to_apply=%region_3.5 | all-reduce | flops 128 | bytes 1024 | tf_op jit(solution)/shard_map/psum | solution.py:76
  284.6 40.5 %all-gather.4 = f32[64,1,128]{2,1,0:T(1,128)S(1)} all-gather(f32[1,1,128]{2,1,0:T(1,128)S(1)} %bitcast.95), channel_id=3, replica_groups=mesh['asset'=64,'rhs'=8] {'asset'}, dimensions={0}, use_global_device_ids=true | all-gather | bytes 33280 | tf_op jit(solution)/shard_map/all_gather | solution.py:48
  325.4 3.3 collective-permute-start.5
  331.2 5.7 fusion.54
  338.9 7.4 %collective-permute-start.6 = (bf16[8,128,128]{2,1,0:T(8,128)(2,1)S(1)}, bf16[8,128,128]{2,1,0:T(8,128)(2,1)}, u32[]{:S(2)}, u32[]{:S(2)}) collective-permute-start(bf16[8,128,128]{2,1,0:T(8,128)(2,1)S(1)} %get-tuple-element.15), channel_id=1, source_target_pairs={{8,0},{16,8},{24,16},{32,24},{40,32},{48,40},{56,48},{64,56},{72,6... | collective-permute-start | bytes 786440 | tf_op jit(solution)/shard_map/ppermute | solution.py:12
  346.5 3.1 gather_fusion.1
  350.1 4.9 fusion.30
  355.2 143.9 %psum.22 = f32[128]{0:T(128)S(1)} all-reduce(f32[128]{0:T(128)S(1)} %multiply_reduce_fusion.2), channel_id=1, replica_groups=mesh['asset'=64,'rhs'=8] {'asset'}, use_global_device_ids=true, to_apply=%region_7.9 | all-reduce | flops 128 | bytes 1024 | tf_op jit(solution)/shard_map/psum | solution.py:76
  499.4 37.8 %all-gather.5 = f32[64,1,128]{2,1,0:T(1,128)S(1)} all-gather(f32[1,1,128]{2,1,0:T(1,128)S(1)} %bitcast.96), channel_id=4, replica_groups=mesh['asset'=64,'rhs'=8] {'asset'}, dimensions={0}, use_global_device_ids=true | all-gather | bytes 33280 | tf_op jit(solution)/shard_map/all_gather | solution.py:48
  537.3 5.2 collective-permute-start.9
  544.4 5.7 fusion.55
  553.2 6.2 collective-permute-start.10
  563.3 5.0 fusion.27
  568.6 143.9 %psum.23 = f32[128]{0:T(128)S(1)} all-reduce(f32[128]{0:T(128)S(1)} %multiply_reduce_fusion), channel_id=1, replica_groups=mesh['asset'=64,'rhs'=8] {'asset'}, use_global_device_ids=true, to_apply=%region_11.13 | all-reduce | flops 128 | bytes 1024 | tf_op jit(solution)/shard_map/psum | solution.py:76
  (53 shorter events, 26.9 us)
Async XLA Ops:
  7.2 49.3 %all-gather.8.cloned.1.call-start = ((), (), s32[]{:S(2)}) async-start(), calls=%async_computation | async-start | bytes 4718592 | tf_op jit(solution)/shard_map/all_gather | solution.py:41
  11.1 77.8 %collective-permute-start.1 = (bf16[1024,128]{1,0:T(8,128)(2,1)S(1)}, bf16[1024,128]{1,0:T(8,128)(2,1)S(1)}, u32[]{:S(2)}, u32[]{:S(2)}) collective-permute-start(bf16[1024,128]{1,0:T(8,128)(2,1)S(1)} %convert_element_type.49), channel_id=1, source_target_pairs={{8,0},{16,8},{24,16},{32,24},{40,32},{48,40},{56,48},{64,56},{72,6... | collective-permute-start | bytes 786440 | tf_op jit(solution)/shard_map/ppermute | solution.py:23
  24.9 63.9 %collective-permute-start = (bf16[1024,128]{1,0:T(8,128)(2,1)S(1)}, bf16[1024,128]{1,0:T(8,128)(2,1)S(1)}, u32[]{:S(2)}, u32[]{:S(2)}) collective-permute-start(bf16[1024,128]{1,0:T(8,128)(2,1)S(1)} %convert_element_type.49), channel_id=1, source_target_pairs={{0,8},{8,16},{16,24},{24,32},{32,40},{40,48},{48,56},{56,64},{64,7... | collective-permute-start | bytes 786440 | tf_op jit(solution)/shard_map/ppermute | solution.py:22
  78.8 15.1 %collective-permute-start.3 = (bf16[8,128,128]{2,1,0:T(8,128)(2,1)}, bf16[8,128,128]{2,1,0:T(8,128)(2,1)}, u32[]{:S(2)}, u32[]{:S(2)}) collective-permute-start(bf16[8,128,128]{2,1,0:T(8,128)(2,1)} %get-tuple-element.18), channel_id=1, source_target_pairs={{504,0},{0,8},{8,16},{16,24},{24,32},{32,40},{40,48},{48,56},{56,6... | collective-permute-start | bytes 786440 | tf_op jit(solution)/shard_map/ppermute | solution.py:12
  82.3 12.5 %collective-permute-start.2 = (bf16[8,128,128]{2,1,0:T(8,128)(2,1)S(1)}, bf16[8,128,128]{2,1,0:T(8,128)(2,1)}, u32[]{:S(2)}, u32[]{:S(2)}) collective-permute-start(bf16[8,128,128]{2,1,0:T(8,128)(2,1)S(1)} %get-tuple-element.17), channel_id=1, source_target_pairs={{8,0},{16,8},{24,16},{32,24},{40,32},{48,40},{56,48},{64,56},{72,6... | collective-permute-start | bytes 786440 | tf_op jit(solution)/shard_map/ppermute | solution.py:12
  94.8 4.9 copy-start
  94.8 5.0 copy-start.1
  325.4 21.0 %collective-permute-start.5 = (bf16[1024,128]{1,0:T(8,128)(2,1)S(1)}, bf16[1024,128]{1,0:T(8,128)(2,1)S(1)}, u32[]{:S(2)}, u32[]{:S(2)}) collective-permute-start(bf16[1024,128]{1,0:T(8,128)(2,1)S(1)} %get-tuple-element.7), channel_id=1, source_target_pairs={{8,0},{16,8},{24,16},{32,24},{40,32},{48,40},{56,48},{64,56},{72,6... | collective-permute-start | bytes 786440 | tf_op jit(solution)/shard_map/ppermute | solution.py:23
  328.7 17.7 %collective-permute-start.4 = (bf16[1024,128]{1,0:T(8,128)(2,1)S(1)}, bf16[1024,128]{1,0:T(8,128)(2,1)S(1)}, u32[]{:S(2)}, u32[]{:S(2)}) collective-permute-start(bf16[1024,128]{1,0:T(8,128)(2,1)S(1)} %get-tuple-element.7), channel_id=1, source_target_pairs={{0,8},{8,16},{16,24},{24,32},{32,40},{40,48},{48,56},{56,64},{64,7... | collective-permute-start | bytes 786440 | tf_op jit(solution)/shard_map/ppermute | solution.py:22
  337.0 12.6 %collective-permute-start.7 = (bf16[8,128,128]{2,1,0:T(8,128)(2,1)S(1)}, bf16[8,128,128]{2,1,0:T(8,128)(2,1)S(1)}, u32[]{:S(2)}, u32[]{:S(2)}) collective-permute-start(bf16[8,128,128]{2,1,0:T(8,128)(2,1)S(1)} %get-tuple-element.16), channel_id=1, source_target_pairs={{504,0},{0,8},{8,16},{16,24},{24,32},{32,40},{40,48},{48,56},{56,6... | collective-permute-start | bytes 786440 | tf_op jit(solution)/shard_map/ppermute | solution.py:12
  338.9 11.1 %collective-permute-start.6 = (bf16[8,128,128]{2,1,0:T(8,128)(2,1)S(1)}, bf16[8,128,128]{2,1,0:T(8,128)(2,1)}, u32[]{:S(2)}, u32[]{:S(2)}) collective-permute-start(bf16[8,128,128]{2,1,0:T(8,128)(2,1)S(1)} %get-tuple-element.15), channel_id=1, source_target_pairs={{8,0},{16,8},{24,16},{32,24},{40,32},{48,40},{56,48},{64,56},{72,6... | collective-permute-start | bytes 786440 | tf_op jit(solution)/shard_map/ppermute | solution.py:12
  537.3 22.1 %collective-permute-start.9 = (bf16[1024,128]{1,0:T(8,128)(2,1)S(1)}, bf16[1024,128]{1,0:T(8,128)(2,1)S(1)}, u32[]{:S(2)}, u32[]{:S(2)}) collective-permute-start(bf16[1024,128]{1,0:T(8,128)(2,1)S(1)} %fusion.34), channel_id=1, source_target_pairs={{8,0},{16,8},{24,16},{32,24},{40,32},{48,40},{56,48},{64,56},{72,6... | collective-permute-start | bytes 786440 | tf_op jit(solution)/shard_map/ppermute | solution.py:23
  542.5 16.9 %collective-permute-start.8 = (bf16[1024,128]{1,0:T(8,128)(2,1)S(1)}, bf16[1024,128]{1,0:T(8,128)(2,1)S(1)}, u32[]{:S(2)}, u32[]{:S(2)}) collective-permute-start(bf16[1024,128]{1,0:T(8,128)(2,1)S(1)} %fusion.34), channel_id=1, source_target_pairs={{0,8},{8,16},{16,24},{24,32},{32,40},{40,48},{48,56},{56,64},{64,7... | collective-permute-start | bytes 786440 | tf_op jit(solution)/shard_map/ppermute | solution.py:22
  550.2 12.3 %collective-permute-start.11 = (bf16[8,128,128]{2,1,0:T(8,128)(2,1)S(1)}, bf16[8,128,128]{2,1,0:T(8,128)(2,1)}, u32[]{:S(2)}, u32[]{:S(2)}) collective-permute-start(bf16[8,128,128]{2,1,0:T(8,128)(2,1)S(1)} %get-tuple-element.14), channel_id=1, source_target_pairs={{504,0},{0,8},{8,16},{16,24},{24,32},{32,40},{40,48},{48,56},{56,6... | collective-permute-start | bytes 786440 | tf_op jit(solution)/shard_map/ppermute | solution.py:12
  553.2 10.2 %collective-permute-start.10 = (bf16[8,128,128]{2,1,0:T(8,128)(2,1)S(1)}, bf16[8,128,128]{2,1,0:T(8,128)(2,1)}, u32[]{:S(2)}, u32[]{:S(2)}) collective-permute-start(bf16[8,128,128]{2,1,0:T(8,128)(2,1)S(1)} %get-tuple-element.13), channel_id=1, source_target_pairs={{8,0},{16,8},{24,16},{32,24},{40,32},{48,40},{56,48},{64,56},{72,6... | collective-permute-start | bytes 786440 | tf_op jit(solution)/shard_map/ppermute | solution.py:12
Sparse Core Ops, SparseCore 0:
  10.7 45.7 all-gather.7
